TPU v7x, 128 devices: a whole 4x4x4 slice. The times are simulated.
128 devices in a mesh: dp: 16 (over z, x), fsdp: 8 (over y, core).
Axes of the slice: x: 4, y: 4, z: 4, core: 2. Of those that a mesh axis runs over, the one named last changes fastest.
Arguments:
- frames: bfloat16 [1024, 64, 1024], P(('dp', 'fsdp')), may hold values from -6 to 6
- lengths: int32 [1024], replicated, may hold values from 8 to 64
- owner: int32 [1024], replicated, may hold values from 0 to 15, as said below
- slot: int32 [1024], replicated, may hold values from 0 to 7, as said below
- w_in: bfloat16 [1024, 2048], P('fsdp'), may hold values from -0.1875 to 0.1875
- kernel: float32 [31, 1024], replicated, may hold values from -1 to 1
- dw_gain: float32 [1024], replicated, may hold values from 0.5 to 1.5
- dw_bias: float32 [1024], replicated, may hold values from -3 to 3
- w_out: bfloat16 [1024, 1024], P('fsdp'), may hold values from -0.1875 to 0.1875
- cotangent: bfloat16 [1024, 64, 1024], P(('dp', 'fsdp')), may hold values from -6 to 6
Outputs:
- out_frames: bfloat16 [1024, 64, 1024], P(('dp', 'fsdp'))
- grad_frames: bfloat16 [1024, 64, 1024], P(('dp', 'fsdp'))
- grad_w_in: float32 [1024, 2048], P('fsdp')
- grad_kernel: float32 [31, 1024], replicated
- grad_gain: float32 [1024], replicated
- grad_bias: float32 [1024], replicated
- grad_w_out: float32 [1024, 1024], P('fsdp')
Inputs may be any that keep to these rules, and one draw needn't show every extreme that they name: Block b lies on the device whose dp index is b // (8 * 8) and whose fsdp index is (b // 8) % 8; its owner has the same fsdp index. The 8 blocks of one device have 8 different owners, and every owner receives exactly 8 blocks. `slot`: the blocks that one owner receives have different slots.
All inputs are finite; a program needn't handle non-finite values.
Results may differ from a plain program's by a relative error of at most 0.014.
Values may be sent and summed in bfloat16 or wider, within the bound.
A program may use at most 128 MiB of HBM per device.

v0:
```python
import math

import jax
import jax.numpy as jnp
from jax import lax
from jax.sharding import PartitionSpec as P


def layer_statistics(values):
    center = values - jnp.mean(values, axis=-1, keepdims=True)
    rstd = lax.rsqrt(jnp.mean(center * center, axis=-1, keepdims=True) + 1e-05)
    return (center * rstd, rstd)


def forward_blocks(frames, lengths, w_in, kernel, dw_gain, dw_bias, w_out):
    element_count, block_number, kernel_width = frames.shape
    frame_mask = (jnp.arange(block_number, dtype=jnp.int32)[None, :] < lengths[:, None]).astype(
        jnp.float32
    )[..., None]
    full_input = frames.astype(jnp.float32)
    normalized_input, inverse_std_input = layer_statistics(full_input)
    input_normed = normalized_input.astype(jnp.bfloat16)
    act = jnp.dot(
        input_normed.reshape(element_count * block_number, kernel_width),
        w_in,
        preferred_element_type=jnp.float32,
    )
    act = act.reshape(element_count, block_number, 2 * kernel_width)
    left_context = act[..., :kernel_width]
    sigmoid_values = jax.nn.sigmoid(act[..., kernel_width:])
    glu = left_context * sigmoid_values * frame_mask
    taps = kernel.shape[0]
    half = (taps - 1) // 2
    padded_frames = jnp.pad(glu, ((0, 0), (half, half), (0, 0)))
    conv = jnp.zeros_like(glu)
    for k in range(taps):
        conv = conv + padded_frames[:, k : k + block_number] * kernel[k]
    centered_normalized, inverse_std_conv = layer_statistics(conv)
    conv_values = centered_normalized * dw_gain + dw_bias
    swish_output = (conv_values * jax.nn.sigmoid(conv_values)).astype(jnp.bfloat16)
    mixed = jnp.dot(
        swish_output.reshape(element_count * block_number, kernel_width),
        w_out,
        preferred_element_type=jnp.float32,
    )
    result = (
        (full_input + mixed.reshape(element_count, block_number, kernel_width)) * frame_mask
    ).astype(jnp.bfloat16)
    saved_residuals = (
        frame_mask,
        normalized_input,
        inverse_std_input,
        input_normed,
        left_context,
        sigmoid_values,
        padded_frames,
        centered_normalized,
        inverse_std_conv,
        conv_values,
        swish_output,
    )
    return (result, saved_residuals)


def backward_blocks(cotangent, saved_residuals, w_in, kernel, dw_gain, w_out):
    (
        frame_mask,
        normalized_input,
        inverse_std_input,
        input_normed,
        left_context,
        sigmoid_values,
        padded_frames,
        centered_normalized,
        inverse_std_conv,
        conv_values,
        swish_output,
    ) = saved_residuals
    element_count, block_number, kernel_width = normalized_input.shape
    taps = kernel.shape[0]
    half = (taps - 1) // 2
    gfull = cotangent.astype(jnp.float32) * frame_mask
    masked = gfull.astype(jnp.bfloat16)
    dswish = lax.dot_general(
        masked.reshape(element_count * block_number, kernel_width),
        w_out,
        (((1,), (1,)), ((), ())),
        preferred_element_type=jnp.float32,
    )
    sigz = jax.nn.sigmoid(conv_values)
    dzval = (
        dswish.reshape(element_count, block_number, kernel_width)
        * sigz
        * (1.0 + conv_values * (1.0 - sigz))
    )
    d_gain = jnp.sum(dzval * centered_normalized, axis=(0, 1))
    d_bias = jnp.sum(dzval, axis=(0, 1))
    dchat = dzval * dw_gain
    dconv = inverse_std_conv * (
        dchat
        - jnp.mean(dchat, axis=-1, keepdims=True)
        - centered_normalized * jnp.mean(dchat * centered_normalized, axis=-1, keepdims=True)
    )
    d_kernel = jnp.stack(
        [jnp.sum(dconv * padded_frames[:, k : k + block_number], axis=(0, 1)) for k in range(taps)]
    )
    dpadded = jnp.pad(dconv, ((0, 0), (half, half), (0, 0)))
    dglu = jnp.zeros_like(dconv)
    for k in range(taps):
        dglu = dglu + dpadded[:, 2 * half - k : 2 * half - k + block_number] * kernel[k]
    dglu = dglu * frame_mask
    dact = jnp.concatenate(
        [dglu * sigmoid_values, dglu * left_context * sigmoid_values * (1.0 - sigmoid_values)],
        axis=-1,
    ).astype(jnp.bfloat16)
    normalized_input_gradient = lax.dot_general(
        dact.reshape(element_count * block_number, 2 * kernel_width),
        w_in,
        (((1,), (1,)), ((), ())),
        preferred_element_type=jnp.float32,
    )
    normalized_input_gradient = normalized_input_gradient.reshape(
        element_count, block_number, kernel_width
    )
    norm_gradient = inverse_std_input * (
        normalized_input_gradient
        - jnp.mean(normalized_input_gradient, axis=-1, keepdims=True)
        - normalized_input
        * jnp.mean(normalized_input_gradient * normalized_input, axis=-1, keepdims=True)
    )
    grad_frames = (norm_gradient + gfull).astype(jnp.bfloat16)
    return (grad_frames, input_normed, dact, swish_output, masked, d_kernel, d_gain, d_bias)


def route(pattern, form, data):
    return jnp.einsum(form, pattern, data, preferred_element_type=jnp.float32).astype(jnp.bfloat16)


def shards(frames, lengths, owner, slot, w_in, kernel, dw_gain, dw_bias, w_out, cotangent):
    n_data = lax.axis_size("dp")
    n_shard = lax.axis_size("fsdp")
    my_data = lax.axis_index("dp")
    my_shard = lax.axis_index("fsdp")
    slots, block_number, kernel_width = frames.shape

    def column_of(table):
        grid = table.reshape(n_data, n_shard, slots)
        return lax.dynamic_index_in_dim(grid, my_shard, 1, keepdims=False)

    owner_col = column_of(owner)
    slot_col = column_of(slot)
    length_col = column_of(lengths)
    owner_mine = lax.dynamic_index_in_dim(owner_col, my_data, 0, keepdims=False)
    peers = jnp.arange(n_data, dtype=jnp.int32)
    outgoing = (owner_mine[None, :] == peers[:, None]).astype(jnp.bfloat16)
    slot_ids = jnp.arange(slots, dtype=jnp.int32)
    matches = (owner_col == my_data)[None, :, :] & (slot_col[None, :, :] == slot_ids[:, None, None])
    incoming = jnp.sum(matches.astype(jnp.int32), axis=2).astype(jnp.bfloat16)
    length_slot = jnp.sum(jnp.where(matches, length_col[None, :, :], 0), axis=(1, 2))
    full_in, full_out = (
        lax.all_gather(w_in, "fsdp", axis=0, tiled=True),
        lax.all_gather(w_out, "fsdp", axis=0, tiled=True),
    )
    arrived = lax.all_to_all(
        route(outgoing, "pj,jtd->ptd", frames), "dp", split_axis=0, concat_axis=0, tiled=True
    )
    local = route(incoming, "sp,ptd->std", arrived)
    out_frames, saved_residuals = forward_blocks(
        local, length_slot, full_in, kernel, dw_gain, dw_bias, full_out
    )
    grad_here, input_normed, dact, swish_output, masked, d_kernel, d_gain, d_bias = backward_blocks(
        cotangent, saved_residuals, full_in, kernel, dw_gain, full_out
    )
    returned = lax.all_to_all(
        route(incoming, "sp,std->ptd", grad_here), "dp", split_axis=0, concat_axis=0, tiled=True
    )
    grad_frames = route(outgoing, "pj,ptd->jtd", returned)
    xn_flat = input_normed.reshape(-1, kernel_width)
    dact_flat = dact.reshape(-1, 2 * kernel_width)
    swish_flat = swish_output.reshape(-1, kernel_width)
    masked_flat = masked.reshape(-1, kernel_width)
    scale = 1.0 / math.sqrt(slots * block_number * n_data * n_shard)
    small_sums = lax.psum((d_kernel, d_gain, d_bias), ("dp", "fsdp"))
    contract = (((0,), (0,)), ((), ()))
    piece = kernel_width // (n_data * n_shard)
    per_shard = kernel_width // n_shard

    def reorder(positions):
        block_id = positions // piece
        return block_id % n_shard * per_shard + block_id // n_shard * piece + positions % piece

    picked = reorder(jnp.arange(piece * lax.axis_size(("dp", "fsdp")), dtype=jnp.int32))
    share_in = lax.psum_scatter(
        lax.dot_general(
            jnp.take(xn_flat, picked, axis=1),
            dact_flat,
            contract,
            preferred_element_type=jnp.float32,
        ),
        ("dp", "fsdp"),
        scatter_dimension=0,
        tiled=True,
    )
    picked = reorder(jnp.arange(piece * lax.axis_size(("dp", "fsdp")), dtype=jnp.int32))
    share_out = lax.psum_scatter(
        lax.dot_general(
            jnp.take(swish_flat, picked, axis=1),
            masked_flat,
            contract,
            preferred_element_type=jnp.float32,
        ),
        ("dp", "fsdp"),
        scatter_dimension=0,
        tiled=True,
    )
    grad_in, grad_out = (
        lax.all_gather(share_in.astype(jnp.bfloat16), "dp", axis=0, tiled=True).astype(
            share_in.dtype
        ),
        lax.all_gather(share_out.astype(jnp.bfloat16), "dp", axis=0, tiled=True).astype(
            share_out.dtype
        ),
    )
    return (
        out_frames,
        grad_frames,
        grad_in * scale,
        small_sums[0] * scale,
        small_sums[1] * scale,
        small_sums[2] * scale,
        grad_out * scale,
    )


def solution(mesh):
    placed = (
        P(("dp", "fsdp"), None, None),
        P(),
        P(),
        P(),
        P("fsdp", None),
        P(),
        P(),
        P(),
        P("fsdp", None),
        P(("dp", "fsdp"), None, None),
    )
    return jax.shard_map(
        shards,
        mesh=mesh,
        in_specs=placed,
        out_specs=(
            P(("dp", "fsdp"), None, None),
            P(("dp", "fsdp"), None, None),
            P("fsdp", None),
            P(),
            P(),
            P(),
            P("fsdp", None),
        ),
        check_vma=False,
    )
```

profile of v0, /device:TPU:0, one launch (start us, length us, event | category | flops | bytes accessed | tf_op | source)
XLA Modules:
  0.0 1566.7 jit_solution(10254423965106041705)
XLA Ops:
  7.2 0.7 all-gather.3.cloned.1.call-update
  7.9 0.8 reshape.169
  8.7 0.9 convolution_convert_fusion.1
  9.7 2.5 copy.164
  12.2 8.1 all-to-all-start
  20.3 0.7 all-gather.5.cloned.1.call-update
  21.9 30.0 %all-to-all-done = bf16[16,64,1024]{2,1,0:T(8,128)(2,1)S(1)} async-done(((bf16[16,64,1024]{2,1,0:T(8,128)(2,1)}), bf16[16,64,1024]{2,1,0:T(8,128)(2,1)S(1)}, u32[]{:S(2)}, u32[]{:S(2)}) %all-to-all-start) | async-done | bytes 2097184 | tf_op jit(solution)/shard_map/all_to_all | solution.py:164
  51.9 1.3 convert_reduce_fusion
  54.1 0.9 copy-done.12
  55.0 4.8 fusion.2
  59.9 1.1 fusion.94
  60.9 0.9 copy-done.2
  61.8 1.6 copy.188
  63.4 9.2 fusion.156
  72.7 1.3 copy-done.8
  74.6 5.5 multiply_reduce_fusion
  80.1 9.7 multiply_reduce_fusion.1
  89.9 3.5 multiply_reduce_fusion.19
  93.4 2.7 stack.127
  97.3 4.0 gather_fusion.1
  101.3 3.3 fusion.106
  104.6 1.2 copy-done.13
  106.9 5.1 gather_fusion
  112.0 16.6 %multiply_convert_fusion.1 = (bf16[8,64,1024]{2,0,1:T(8,128)(2,1)S(1)}, f32[8,64,1024]{2,0,1:T(8,128)S(1)}) fusion(f32[8,64,2048]{2,0,1:T(8,128)} %copy-done.2, f32[8,64]{0,1:T(8,128)S(1)} %fusion.123, f32[1024]{0:T(1024)S(1)} %bitcast.138, f32[1024]{0:T(1024)S(1)} %bitcast.140, f32[1024]{0:T(1024)S(1)} %bitcast.144, f32[1024]{0:T(1024)S(1)} %bitcast.146, ...), kind=kLoop, calls=%fused_computation.194 | loop fusion | flops 35127296 | bytes 7469056 | tf_op jit(solution)/shard_map/convert.4
  128.6 0.9 multiply_convert_fusion
  130.7 5.6 fusion.81
  136.4 1.2 copy-done.11
  137.7 2.0 copy-done.25
  139.8 3.0 fusion.159
  142.9 1.3 fusion.9
  144.2 2.0 convolution_convert_fusion
  146.2 2.5 copy.180
  148.8 3.9 all-to-all-start.1
  152.7 3.2 fusion.16
  155.9 1.5 copy.189
  157.4 81.0 %all-reduce.2 = (f32[1024]{0:T(1024)S(1)}, f32[1024]{0:T(1024)S(1)}) all-reduce(f32[1024]{0:T(1024)S(1)} %get-tuple-element.50, f32[1024]{0:T(1024)S(1)} %get-tuple-element.84), channel_id=1, replica_groups=mesh['dp'=16,'fsdp'=8] {'dp','fsdp'}, use_global_device_ids=true, to_apply=%region_44.46 | all-reduce | flops 2048 | bytes 16384 | tf_op jit(solution)/shard_map/psum | solution.py:183
  239.6 8.9 all-reduce.5.cloned.1.call-done
  248.5 1.6 broadcast_multiply_fusion
  250.1 1.3 fusion.100
  251.4 1.5 copy.190
  252.9 637.9 %reduce-scatter.5.cloned.1.call-done = f32[8,1024]{1,0:T(8,128)} async-done(((f32[1024,1024]{1,0:T(8,128)}), f32[8,1024]{1,0:T(8,128)}) %reduce-scatter.5.cloned.1.call-update) | async-done | bytes 32784 | tf_op jit(solution)/shard_map/reduce_scatter | solution.py:205
  890.8 0.8 convert_element_type.81
  891.6 20.8 %all_gather.15 = bf16[128,1024]{1,0:T(8,128)(2,1)S(1)} all-gather(bf16[8,1024]{1,0:T(8,128)(2,1)S(1)} %convert_element_type.81), channel_id=1, replica_groups=mesh['dp'=16,'fsdp'=8] {'dp'}, dimensions={0}, use_global_device_ids=true | all-gather | bytes 278528 | tf_op jit(solution)/shard_map/all_gather | solution.py:220
  912.4 0.8 convert_multiply_fusion.2
  913.3 623.8 %reduce-scatter.3.cloned.1.call-done = f32[8,2048]{1,0:T(8,128)} async-done(((f32[1024,2048]{1,0:T(8,128)}), f32[8,2048]{1,0:T(8,128)}) %reduce-scatter.3.cloned.1.call-update) | async-done | bytes 65552 | tf_op jit(solution)/shard_map/reduce_scatter | solution.py:193
  1537.1 0.8 convert_element_type.79
  1537.9 21.0 %all_gather.14 = bf16[128,2048]{1,0:T(8,128)(2,1)S(1)} all-gather(bf16[8,2048]{1,0:T(8,128)(2,1)S(1)} %convert_element_type.79), channel_id=1, replica_groups=mesh['dp'=16,'fsdp'=8] {'dp'}, dimensions={0}, use_global_device_ids=true | all-gather | bytes 557056 | tf_op jit(solution)/shard_map/all_gather | solution.py:217
  1558.9 1.1 convert_multiply_fusion.1
  (95 shorter events, 7.5 us)
Async XLA Ops:
  7.2 1.6 copy-start
  7.2 46.9 %all-gather.3.cloned.1.call-start = ((), (), s32[]{:S(2)}) async-start(), calls=%async_computation.4 | async-start | bytes 4718592 | tf_op jit(solution)/shard_map/all_gather | solution.py:161
  12.2 8.9 copy-start.23
  12.2 9.0 copy-start.24
  12.2 9.7 copy-start.21
  12.2 39.8 %all-to-all-start = ((bf16[16,64,1024]{2,1,0:T(8,128)(2,1)}), bf16[16,64,1024]{2,1,0:T(8,128)(2,1)S(1)}, u32[]{:S(2)}, u32[]{:S(2)}) async-start(bf16[16,64,1024]{2,1,0:T(8,128)(2,1)} %copy.164), calls=%async_computation | async-start | bytes 4194304 | tf_op jit(solution)/shard_map/all_to_all | solution.py:164
  20.3 54.0 %all-gather.5.cloned.1.call-start = ((), (), s32[]{:S(2)}) async-start(), calls=%async_computation.5 | async-start | bytes 2359296 | tf_op jit(solution)/shard_map/all_gather | solution.py:162
  21.0 227.5 %all-reduce.5.cloned.1.call-start = ((), (), s32[]{:S(2)}) async-start(), calls=%async_computation.7 | async-start | bytes 262144 | tf_op jit(solution)/shard_map/psum | solution.py:183
  53.3 6.6 copy-start.4
  54.0 1.0 copy-start.12
  55.0 4.8 copy-start.16
  59.8 1.9 copy-start.2
  61.8 1.6 copy-start.14
  72.6 1.3 copy-start.8
  72.6 2.0 copy-start.15
  72.6 2.0 copy-start.22
  72.6 2.0 copy-start.26
  74.6 5.5 copy-start.9
  89.9 3.5 copy-start.6
  89.9 6.3 copy-start.19
  96.1 794.8 %reduce-scatter.5.cloned.1.call-start = ((), (), s32[]{:S(2)}) async-start(), calls=%async_computation.8 | async-start | bytes 4227072 | tf_op jit(solution)/shard_map/reduce_scatter | solution.py:205
  97.3 4.0 copy-start.20
  104.5 1.2 copy-start.13
  104.6 1432.5 %reduce-scatter.3.cloned.1.call-start = ((), (), s32[]{:S(2)}) async-start(), calls=%async_computation.6 | async-start | bytes 8454144 | tf_op jit(solution)/shard_map/reduce_scatter | solution.py:193
  106.9 5.1 copy-start.7
  112.0 16.6 %copy-start.3 = (f32[8,64,2048]{2,0,1:T(8,128)S(1)}, f32[8,64,2048]{2,0,1:T(8,128)}, u32[]{:S(2)}) copy-start(f32[8,64,2048]{2,0,1:T(8,128)} %copy-done.2) | copy-start | bytes 12582916
  128.6 1.5 copy-start.10
  129.5 1.2 copy-start.18
  136.3 1.2 copy-start.11
  137.6 2.2 copy-start.25
  139.8 3.1 copy-start.5
  142.8 1.3 copy-start.17
  148.8 101.4 %all-to-all-start.1 = ((bf16[16,64,1024]{2,1,0:T(8,128)(2,1)}), bf16[16,64,1024]{2,1,0:T(8,128)(2,1)S(1)}, u32[]{:S(2)}, u32[]{:S(2)}) async-start(bf16[16,64,1024]{2,1,0:T(8,128)(2,1)} %copy.180), calls=%async_computation.1 | async-start | bytes 4194304 | tf_op jit(solution)/shard_map/all_to_all | solution.py:174
  251.4 1308.6 %copy-start.1 = (bf16[8,64,1024]{2,1,0:T(8,128)(2,1)S(1)}, bf16[8,64,1024]{2,1,0:T(8,128)(2,1)}, u32[]{:S(2)}) copy-start(bf16[8,64,1024]{2,1,0:T(8,128)(2,1)} %param.12) | copy-start | bytes 3145732
Sparse Core Ops, SparseCore 0:
  9.7 34.5 all-gather.2
  46.1 25.1 all-gather.4
  96.2 152.2 all-reduce.4
  250.9 639.9 reduce-scatter.4
  893.1 643.9 reduce-scatter.2
where the time goes:
time: 1570 us
  waiting for transfers between devices  1300 us (83%)
  blocking collectives  123 us (8%)
  other arithmetic  50.2 us (3%)
  local copies, waits for them, and re-layouts  34 us (2%)
  matrix products  30.9 us (2%)
    reduce_scatter x1, waiting for transfers between devices, shards(): lax.psum_scatter(lax.dot_general(jnp.take(swish_flat, picked, axis=1), ma...  638 us
    reduce_scatter x1, waiting for transfers between devices, shards(): lax.psum_scatter(lax.dot_general(jnp.take(xn_flat, picked, axis=1), dact_...  624 us
    psum x1, blocking collectives, shards(): small_sums = lax.psum((d_kernel, d_gain, d_bias), ('dp', 'fsdp'))  81 us
  transfers between devices with their start and end apart: 7, of which 4 were waited for; matrix products, arithmetic and copies ran while one was open for 5% of the time, Pallas kernels for 0%

commit v1 on v0

v1 whole, which is shorter than its diff:
```python
import math
import types

import jax
import jax.numpy as jnp
from jax import lax
from jax.experimental import pallas as pl
from jax.experimental.pallas import tpu as pltpu
from jax.sharding import PartitionSpec as P

MESH = pl.DeviceIdType.MESH

LANES = 128
CHUNK = 16
PIECE = 256
BLOCK = 64
RING = 4
EPS = 1e-05
NT = (((1,), (1,)), ((), ()))
TN = (((0,), (0,)), ((), ()))
BF16 = jnp.bfloat16
F32 = jnp.float32


def lanes_of(i, width=LANES):
    return pl.ds(pl.multiple_of(i * width, width), width)


def statistics(values):
    center = values - jnp.mean(values, axis=-1, keepdims=True)
    rstd = lax.rsqrt(jnp.mean(center * center, axis=-1, keepdims=True) + EPS)
    return center * rstd, rstd


def logistic(v):
    return 1.0 / (1.0 + jnp.exp(-v))


def order_matrix(rows, slots, to_time):
    r = lax.broadcasted_iota(jnp.int32, (rows, rows), 0)
    c = lax.broadcasted_iota(jnp.int32, (rows, rows), 1)
    frames = rows // slots
    if to_time:
        place = (r % slots) * frames + r // slots
    else:
        place = (r % frames) * slots + r // frames
    return jnp.where(c == place, 1.0, 0.0).astype(BF16)


def prepare(m):
    m.small[...] = jnp.zeros_like(m.small)
    taps, slots, width = m.spread.shape
    half = (taps - 1) // 2
    frames = m.glu.shape[0] - 2 * half
    for k in range(taps):
        m.spread[k] = jnp.broadcast_to(m.taps[k : k + 1, :], (slots, width))
    m.to_time[...] = order_matrix(m.xn.shape[0], slots, True)
    m.to_block[...] = order_matrix(m.xn.shape[0], slots, False)
    edge = jnp.zeros((half, slots, width), F32)
    for ref in (m.glu, m.dconv):
        ref[pl.ds(0, half)] = edge
        ref[pl.ds(half + frames, half)] = edge


def norm_input(m):
    rows, width = m.xp.shape

    @pl.loop(0, width // PIECE)
    def _(j):
        c = lanes_of(j, PIECE)
        m.xp[:, c] = jnp.dot(m.to_time[...], m.x[:, c], preferred_element_type=F32).astype(BF16)

    @pl.loop(0, rows // BLOCK)
    def _(i):
        r = pl.ds(pl.multiple_of(i * BLOCK, BLOCK), BLOCK)
        m.xn[r, :] = statistics(m.xp[r, :].astype(F32))[0].astype(BF16)


def gate_chunk(m, j):
    rows, width = m.xn.shape
    slots = m.limit.shape[0]
    frames = rows // slots
    half = (m.spread.shape[0] - 1) // 2
    c = pl.ds(j * PIECE, PIECE)
    left = jnp.dot(m.xn[...], m.w_in[:, pl.ds(2 * j * PIECE, PIECE)], preferred_element_type=F32)
    gate = jnp.dot(m.xn[...], m.w_in[:, pl.ds((2 * j + 1) * PIECE, PIECE)], preferred_element_type=F32)
    sig = logistic(gate)
    m.sig[:, c] = sig
    time = lax.broadcasted_iota(jnp.int32, (frames, slots, PIECE), 0)
    limit = jnp.concatenate([m.limit[...]] * (PIECE // LANES), axis=1)
    glu = (left * sig).reshape(frames, slots, PIECE)
    m.glu[pl.ds(half, frames), :, c] = jnp.where(time < limit[None], glu, 0.0)


def slide(padded, spread, start, lanes, flip):
    taps = spread.shape[0]
    acc = None
    for k in range(taps):
        weight = spread[taps - 1 - k if flip else k, :, lanes]
        term = weight[None] * padded[pl.ds(start + k, CHUNK), :, lanes]
        acc = term if acc is None else acc + term
    return acc


def conv_chunk(m, j):
    rows, width = m.xn.shape
    slots = m.limit.shape[0]
    steps = rows // slots // CHUNK

    @pl.loop(0, PIECE // LANES * steps)
    def _(i):
        c = lanes_of(j * (PIECE // LANES) + i // steps)
        t = i % steps
        acc = slide(m.glu, m.spread, t * CHUNK, c, False)
        r = pl.ds(pl.multiple_of(t * CHUNK * slots, CHUNK * slots), CHUNK * slots)
        m.chat[r, c] = acc.reshape(CHUNK * slots, LANES)


def norm_conv(m):
    rows, width = m.xn.shape

    @pl.loop(0, rows // BLOCK)
    def _(i):
        r = pl.ds(pl.multiple_of(i * BLOCK, BLOCK), BLOCK)
        chat, rstd = statistics(m.chat[r, :])
        m.chat[r, :] = chat
        m.rstd[r, :] = jnp.broadcast_to(rstd, (BLOCK, LANES))
        z = chat * m.gain[...] + m.bias[...]
        m.sw[r, :] = (z * logistic(z)).astype(BF16)


def mix_out(m):
    rows, width = m.xn.shape
    slots = m.limit.shape[0]
    frames = rows // slots

    @pl.loop(0, width // PIECE)
    def _(j):
        c = lanes_of(j, PIECE)
        mixed = jnp.dot(m.sw[...], m.w_out[:, c], preferred_element_type=F32)
        time = lax.broadcasted_iota(jnp.int32, (frames, slots, PIECE), 0)
        limit = jnp.concatenate([m.limit[...]] * (PIECE // LANES), axis=1)
        out = (m.xp[:, c].astype(F32) + mixed).reshape(frames, slots, PIECE)
        m.dx[:, c] = jnp.where(time < limit[None], out, 0.0).reshape(rows, PIECE).astype(BF16)


def untime(m, dst):
    slots, frames, width = dst.shape

    @pl.loop(0, width // PIECE)
    def _(j):
        c = lanes_of(j, PIECE)
        line = jnp.dot(m.to_block[...], m.dx[:, c], preferred_element_type=F32).astype(BF16)
        for b in range(slots):
            dst[b, :, c] = line[b * frames : (b + 1) * frames, :]


def mask_cotangent(m):
    rows, width = m.xn.shape
    slots = m.limit.shape[0]
    frames = rows // slots

    @pl.loop(0, width // PIECE)
    def _(j):
        c = lanes_of(j, PIECE)
        g = jnp.dot(m.to_time[...], m.dx[:, c], preferred_element_type=F32)
        time = lax.broadcasted_iota(jnp.int32, (frames, slots, PIECE), 0)
        limit = jnp.concatenate([m.limit[...]] * (PIECE // LANES), axis=1)
        g = jnp.where(time < limit[None], g.reshape(frames, slots, PIECE), 0.0)
        m.gm[:, c] = g.reshape(rows, PIECE).astype(BF16)


def norm_conv_back(m):
    rows, width = m.xn.shape
    taps, slots, _ = m.spread.shape
    half = (taps - 1) // 2
    steps = BLOCK // slots
    m.sums[...] = jnp.zeros_like(m.sums)

    @pl.loop(0, width // PIECE)
    def _(j):
        c = lanes_of(j, PIECE)
        m.wide[:, c] = lax.dot_general(m.gm[...], m.w_out[c, :], NT, preferred_element_type=F32)

    @pl.loop(0, rows // BLOCK)
    def _(i):
        r = pl.ds(pl.multiple_of(i * BLOCK, BLOCK), BLOCK)
        ds = m.wide[r, :]
        chat = m.chat[r, :]
        gain = m.gain[...]
        z = chat * gain + m.bias[...]
        sigz = logistic(z)
        dz = ds * sigz * (1.0 + z * (1.0 - sigz))
        m.sums[0] += jnp.sum((dz * chat).reshape(steps, slots, width), axis=0)
        m.sums[1] += jnp.sum(dz.reshape(steps, slots, width), axis=0)
        dchat = dz * gain
        m1 = jnp.mean(dchat, axis=-1, keepdims=True)
        m2 = jnp.mean(dchat * chat, axis=-1, keepdims=True)
        dconv = m.rstd[r, :][:, :1] * (dchat - m1 - chat * m2)
        m.dconv[pl.ds(half + i * steps, steps)] = dconv.reshape(steps, slots, width)


def conv_back(m):
    rows, width = m.xn.shape
    taps, slots, _ = m.spread.shape
    frames = rows // slots
    half = (taps - 1) // 2
    steps = frames // CHUNK

    @pl.loop(0, width // LANES * steps)
    def _(i):
        l = i // steps
        t = i % steps
        c = lanes_of(l)
        acc = slide(m.dconv, m.spread, t * CHUNK, c, True)
        r = pl.ds(pl.multiple_of(t * CHUNK * slots, CHUNK * slots), CHUNK * slots)
        near = lax.broadcasted_iota(jnp.int32, (CHUNK, slots, LANES), 0) + t * CHUNK
        dglu = jnp.where(near < m.limit[...][None], acc, 0.0).reshape(CHUNK * slots, LANES)
        sig = m.sig[r, c]
        glu = m.glu[pl.ds(half + t * CHUNK, CHUNK), :, c].reshape(CHUNK * slots, LANES)
        place = (l // 2) * 4 + l % 2
        m.da[r, lanes_of(place)] = (dglu * sig).astype(BF16)
        m.da[r, lanes_of(place + 2)] = (dglu * glu * (1.0 - sig)).astype(BF16)


def taps_back(m):
    rows, width = m.xn.shape
    taps, slots, _ = m.spread.shape
    frames = rows // slots
    half = (taps - 1) // 2
    lanes_q = width // 8 // LANES
    step = 8

    @pl.loop(0, width // LANES)
    def _(l):
        c = lanes_of(l)
        for low in range(0, taps, 16):
            count = min(16, taps - low)

            def body(t, acc, low=low, count=count):
                base = t * step
                out = []
                d = m.dconv[pl.ds(half + base, step), :, c]
                for k in range(count):
                    row = m.glu[pl.ds(base + low + k, step), :, c]
                    out.append(acc[k] + jnp.sum(d * row, axis=0))
                return tuple(out)

            acc = lax.fori_loop(0, frames // step, body,
                                tuple(jnp.zeros((slots, LANES), F32) for _ in range(count)))
            for k in range(count):
                m.small[l // 4, l % 4, pl.ds(low + k, 1), :] = jnp.sum(acc[k], axis=0, keepdims=True)
        for k in range(2):
            m.small[l // 4, l % 4, pl.ds(taps + k, 1), :] = jnp.sum(m.sums[k, :, c], axis=0, keepdims=True)


def norm_input_back(m):
    rows, width = m.xn.shape

    @pl.loop(0, width // PIECE)
    def _(j):
        c = lanes_of(j, PIECE)
        m.wide[:, c] = lax.dot_general(m.da[...], m.w_in[c, :], NT, preferred_element_type=F32)

    @pl.loop(0, rows // BLOCK)
    def _(i):
        r = pl.ds(pl.multiple_of(i * BLOCK, BLOCK), BLOCK)
        dxn = m.wide[r, :]
        xhat, rstd = statistics(m.xp[r, :].astype(F32))
        m1 = jnp.mean(dxn, axis=-1, keepdims=True)
        m2 = jnp.mean(dxn * xhat, axis=-1, keepdims=True)
        dx = rstd * (dxn - m1 - xhat * m2) + m.gm[r, :].astype(F32)
        m.dx[r, :] = dx.astype(BF16)


def save_pieces(m, y, k, b, part):
    size = m.pieces.shape[4]
    for core in range(2):
        for a in range(RING):
            low = (core * RING + a) * size
            m.pieces[core, k, y, a * RING + b] = part[low : low + size, :]


def weight_in_grad(m):
    @pl.loop(0, RING)
    def _(y):
        xn = m.xn[:, lanes_of(y, PIECE)]
        for q in range(8):
            part = lax.dot_general(xn, m.da[:, pl.ds(q * PIECE, PIECE)], TN, preferred_element_type=F32)
            save_pieces(m, y, q % 2, q // 2, part.astype(BF16))


def weight_out_grad(m):
    @pl.loop(0, RING)
    def _(y):
        sw = m.sw[:, lanes_of(y, PIECE)]
        for b in range(RING):
            part = lax.dot_general(sw, m.gm[:, pl.ds(b * PIECE, PIECE)], TN, preferred_element_type=F32)
            save_pieces(m, y, 2, b, part.astype(BF16))


def module_kernel(scale, names, *refs):
    m = types.SimpleNamespace(**dict(zip(names, refs)))
    data = lax.axis_index("dp")
    shard = lax.axis_index("fsdp")
    y, core = shard // 2, shard % 2
    n_data = m.sendb.shape[0]
    slots, frames, width = m.cot.shape
    rows = slots * frames
    per = m.w_in_shard.shape[0]
    ring_y = range(1, RING)
    ring_d = range(1, n_data)

    def at_y(offset):
        return lax.rem(y + offset, RING)

    def at_d(offset):
        return lax.rem(data + offset, n_data)

    partner = (data, y * 2 + (1 - core))

    def peer_y(offset):
        return (data, at_y(offset) * 2 + core)

    def peer_d(offset):
        return (at_d(offset), shard)

    barrier = pltpu.get_barrier_semaphore()
    pl.semaphore_signal(barrier, inc=1, device_id=partner, device_id_type=MESH)
    for o in ring_y:
        pl.semaphore_signal(barrier, inc=1, device_id=peer_y(o), device_id_type=MESH)
    for o in ring_d:
        pl.semaphore_signal(barrier, inc=1, device_id=peer_d(o), device_id_type=MESH)

    pending = []

    def push(src, dst, sems, place, device, keep=True):
        copy = pltpu.make_async_remote_copy(
            src_ref=src, dst_ref=dst, send_sem=sems[0].at[place], recv_sem=sems[1].at[place],
            device_id=device, device_id_type=MESH)
        copy.start()
        if keep:
            pending.append(copy)
        return copy

    def arrive(copies):
        for copy in copies:
            copy.wait_recv()

    def wide(a):
        return a.astype(F32)

    mine = pl.ds(pl.multiple_of(shard * per, per), per)
    chunks = width // PIECE
    for j in range(chunks):
        m.w_in[mine, pl.ds(2 * j * PIECE, PIECE)] = m.w_in_shard[:, pl.ds(j * PIECE, PIECE)]
        m.w_in[mine, pl.ds((2 * j + 1) * PIECE, PIECE)] = m.w_in_shard[:, pl.ds(width + j * PIECE, PIECE)]
    m.w_out[mine, :] = m.w_out_shard[...]

    @pl.loop(0, n_data)
    def _(p):
        m.sendb[p] = m.cot[m.slot_for[p]]

    pl.semaphore_wait(barrier, 1 + len(ring_y) + len(ring_d))

    def part(j, owner_y):
        r = pl.ds(pl.multiple_of((owner_y * 2 + core) * per, per), per)
        if j < chunks:
            return m.w_in.at[r, pl.ds(2 * j * PIECE, 2 * PIECE)]
        return m.w_out.at[r, :]

    weights, passed = [], []
    for j in range(chunks + 1):
        src = part(j, y)
        weights.append([push(src, src, m.weight_sems, (j, o - 1), peer_y(o)) for o in ring_y])
        passed.append([push(src, src, m.pass_sems, (j, 0), partner)])

    def exchange(dst, sems):
        copies = [push(m.sendb.at[at_d(o)], dst.at[data], sems, o - 1, peer_d(o), False) for o in ring_d]
        dst[data] = m.sendb[data]
        return copies

    cot_copies = exchange(m.cot_recv, m.cot_sems)

    prepare(m)
    norm_input(m)

    def weights_ready(j):
        for o in ring_y:
            weights[j][o - 1].wait_recv()
            src = part(j, lax.rem(y + RING - o, RING))
            passed[j].append(push(src, src, m.pass_sems, (j, o), partner))
        arrive(passed[j])

    for j in range(chunks):
        weights_ready(j)
        gate_chunk(m, j)
        conv_chunk(m, j)
    norm_conv(m)

    arrive(cot_copies)
    for b in range(slots):
        m.dx[pl.ds(b * frames, frames), :] = m.cot_recv[m.owner[b]]
    mask_cotangent(m)

    weights_ready(chunks)
    mix_out(m)
    untime(m, m.lines)
    for copy in cot_copies:
        copy.wait_send()

    @pl.loop(0, n_data)
    def _(p):
        m.sendb[p] = m.lines[m.block_for[p]]

    out_copies = exchange(m.out_recv, m.out_sems)
    pending.extend(out_copies)

    def core_start(k):
        return [push(m.pieces.at[1 - core, k], m.core_recv.at[k], m.core_sems, k, partner)]

    def first(k, copies):
        arrive(copies)

        @pl.loop(0, RING)
        def _(a):
            m.pieces[core, k, a] = (wide(m.pieces[core, k, a]) + wide(m.core_recv[k, a])).astype(BF16)

        if k != 1:
            return [push(m.pieces.at[core, k, at_y(o)], m.recv_y.at[k // 2, o - 1], m.sum_y_sems,
                         (k, o - 1), peer_y(o)) for o in ring_y]
        return [push(m.pieces.at[core, k, :, at_d(o)], m.recv_d.at[o - 1], m.sum_d_sems,
                     (k, o - 1), peer_d(o)) for o in ring_d]

    def second(k, copies):
        arrive(copies)
        if k != 1:
            @pl.loop(0, n_data)
            def _(d):
                acc = wide(m.pieces[core, k, y, d])
                for o in ring_y:
                    acc = acc + wide(m.recv_y[k // 2, o - 1, d])
                m.pieces[core, k, y, d] = acc.astype(BF16)

            return [push(m.pieces.at[core, k, y, at_d(o)], m.last_d.at[k // 2, o - 1], m.sum_d_sems,
                         (k, o - 1), peer_d(o)) for o in ring_d]

        @pl.loop(0, RING)
        def _(a):
            acc = wide(m.pieces[core, k, a, data])
            for o in ring_d:
                acc = acc + wide(m.recv_d[o - 1, a])
            m.pieces[core, k, a, data] = acc.astype(BF16)

        return [push(m.pieces.at[core, k, at_y(o), data], m.last_y.at[o - 1], m.sum_y_sems,
                     (k, o - 1), peer_y(o)) for o in ring_y]

    def third(k, copies):
        arrive(copies)
        acc = wide(m.pieces[core, k, y, data])
        if k != 1:
            for o in ring_d:
                acc = acc + wide(m.last_d[k // 2, o - 1])
        else:
            for o in ring_y:
                acc = acc + wide(m.last_y[o - 1])
        m.fin[k, data] = acc.astype(BF16)
        return [push(m.fin.at[k, data], m.fin.at[k, data], m.fin_sems, (k, o - 1), peer_d(o)) for o in ring_d]

    def last(k, copies):
        arrive(copies)
        size, cols = m.fin.shape[2], m.fin.shape[3]
        for a in range(RING):
            for b in range(RING):
                piece = wide(m.fin[k, a * RING + b]) * scale
                r = pl.ds(a * size, size)
                if k < 2:
                    m.grad_in[r, pl.ds((k * RING + b) * cols, cols)] = piece
                else:
                    m.grad_out[r, pl.ds(b * cols, cols)] = piece

    weight_out_grad(m)
    two = core_start(2)
    norm_conv_back(m)
    two = first(2, two)
    conv_back(m)
    two = second(2, two)
    taps_back(m)

    small = [push(m.small.at[1 - core], m.small_core, m.small_sems, 0, partner)]
    two = third(2, two)
    weight_in_grad(m)
    zero, one = core_start(0), core_start(1)

    arrive(small)
    m.small_core[...] = m.small_core[...] + m.small[core]
    m.small_y[y] = m.small_core[y]
    small = [push(m.small_core.at[at_y(o)], m.small_y.at[y], m.small_sems, o, peer_y(o)) for o in ring_y]

    zero = first(0, zero)
    one = first(1, one)

    arrive(small)
    m.small_d[data] = (m.small_y[0] + m.small_y[1]) + (m.small_y[2] + m.small_y[3])
    small = [push(m.small_d.at[data], m.small_d.at[data], m.small_d_sems, o - 1, peer_d(o)) for o in ring_d]

    norm_input_back(m)
    untime(m, m.grad_frames)
    last(2, two)

    arrive(small)
    total = m.small_d[0]
    for d in range(1, n_data):
        total = total + m.small_d[d]
    m.small_all[core, y] = total
    mine = m.small_all.at[core, y]
    small = [push(mine, mine, m.small_sems, RING + o, peer_y(o)) for o in ring_y]

    zero = second(0, zero)
    one = second(1, one)
    arrive(small)
    half = m.small_all.at[core]
    small = [push(half, half, m.small_sems, 2 * RING, partner)]

    zero = third(0, zero)
    one = third(1, one)

    arrive(out_copies)

    @pl.loop(0, slots)
    def _(s):
        m.out_frames[s] = m.out_recv[m.source_of[s]]

    arrive(small)
    lanes = m.small_all.shape[3]
    for a in range(2):
        for b in range(RING):
            m.small_out[:, pl.ds((a * RING + b) * lanes, lanes)] = m.small_all[a, b] * scale
    last(0, zero)
    last(1, one)
    for copy in pending:
        copy.wait_send()


def module_call(scale, tables, frames, cotangent, limit, w_in, taps, gain, bias, w_out, n_data):
    slots, count, width = frames.shape
    rows = slots * count
    k = taps.shape[0]
    lines = -(-(k + 2) // 8) * 8
    size, cols = width // 32, width // RING
    lanes = width // 8
    shape = jax.ShapeDtypeStruct
    dma = pltpu.SemaphoreType.DMA
    inputs = dict(
        slot_for=tables[0], owner=tables[1], block_for=tables[2], source_of=tables[3],
        x=frames.reshape(rows, width), cot=cotangent, limit=limit, w_in_shard=w_in, taps=taps,
        gain=gain, bias=bias, w_out_shard=w_out)
    outputs = dict(
        out_frames=shape((slots, count, width), BF16),
        grad_frames=shape((slots, count, width), BF16),
        grad_in=shape((width // 8, 2 * width), F32),
        grad_out=shape((width // 8, width), F32),
        small_out=shape((lines, width), F32))
    buffers = dict(
        w_in=((width, 2 * width), BF16), w_out=((width, width), BF16),
        xp=((rows, width), BF16), xn=((rows, width), BF16), sig=((rows, width), F32),
        chat=((rows, width), F32), rstd=((rows, LANES), F32), sw=((rows, width), BF16),
        glu=((count + k - 1, slots, width), F32), dconv=((count + k - 1, slots, width), F32),
        spread=((k, slots, width), F32), gm=((rows, width), BF16), da=((rows, 2 * width), BF16),
        dx=((rows, width), BF16), wide=((rows, width), F32), sums=((2, slots, width), F32),
        to_time=((rows, rows), BF16), to_block=((rows, rows), BF16),
        lines=((slots, count, width), BF16), sendb=((n_data, count, width), BF16),
        cot_recv=((n_data, count, width), BF16), out_recv=((n_data, count, width), BF16),
        pieces=((2, 3, RING, n_data, size, cols), BF16),
        core_recv=((3, RING, n_data, size, cols), BF16),
        recv_y=((2, RING - 1, n_data, size, cols), BF16),
        recv_d=((n_data - 1, RING, size, cols), BF16),
        last_d=((2, n_data - 1, size, cols), BF16), last_y=((RING - 1, size, cols), BF16),
        fin=((3, n_data, size, cols), BF16),
        small=((2, RING, lines, lanes), F32), small_core=((RING, lines, lanes), F32),
        small_y=((RING, lines, lanes), F32), small_d=((n_data, lines, lanes), F32),
        small_all=((2, RING, lines, lanes), F32))
    pairs = dict(
        weight_sems=(5, RING - 1), pass_sems=(5, RING), cot_sems=(n_data - 1,), out_sems=(n_data - 1,),
        core_sems=(3,), sum_y_sems=(3, RING - 1), sum_d_sems=(3, n_data - 1), fin_sems=(3, n_data - 1),
        small_sems=(2 * RING + 1,), small_d_sems=(n_data - 1,))
    names = list(inputs) + list(outputs) + list(buffers)
    vmem = pl.BlockSpec(memory_space=pltpu.VMEM)
    smem = pl.BlockSpec(memory_space=pltpu.SMEM)

    def body(*refs):
        plain, sems = refs[: len(names)], refs[len(names) :]
        both = [(sems[2 * i], sems[2 * i + 1]) for i in range(len(pairs))]
        module_kernel(scale, names + list(pairs), *plain, *both)

    return pl.pallas_call(
        body,
        out_shape=tuple(outputs.values()),
        in_specs=[smem] * 4 + [vmem] * (len(inputs) - 4),
        out_specs=(vmem,) * len(outputs),
        scratch_shapes=[pltpu.VMEM(*b) for b in buffers.values()]
        + [dma(s) for s in pairs.values() for _ in range(2)],
        compiler_params=pltpu.CompilerParams(
            collective_id=0, has_side_effects=True, vmem_limit_bytes=VMEM_LIMIT),
        name="conv_module",
    )(*inputs.values())


VMEM_LIMIT = 63 * 2**20


def shards(frames, lengths, owner, slot, w_in, kernel, dw_gain, dw_bias, w_out, cotangent):
    n_data = lax.axis_size("dp")
    n_shard = lax.axis_size("fsdp")
    my_data = lax.axis_index("dp")
    my_shard = lax.axis_index("fsdp")
    slots, count, width = frames.shape

    def column_of(table):
        grid = table.reshape(n_data, n_shard, slots)
        return lax.dynamic_index_in_dim(grid, my_shard, 1, keepdims=False)

    owner_col = column_of(owner)
    slot_col = column_of(slot)
    owner_mine = lax.dynamic_index_in_dim(owner_col, my_data, 0, keepdims=False)
    length_mine = lax.dynamic_index_in_dim(column_of(lengths), my_data, 0, keepdims=False)
    here = owner_col == my_data
    slot_for = jnp.sum(jnp.where(here, slot_col, 0), axis=1)
    slot_ids = jnp.arange(slots, dtype=jnp.int32)
    peers = jnp.arange(n_data, dtype=jnp.int32)
    block_for = jnp.sum(jnp.where(owner_mine[None, :] == peers[:, None], slot_ids[None, :], 0), axis=1)
    matches = here[None, :, :] & (slot_col[None, :, :] == slot_ids[:, None, None])
    source_of = jnp.sum(jnp.where(matches, peers[None, :, None], 0), axis=(1, 2))
    limit = jnp.broadcast_to(length_mine[:, None], (slots, LANES))
    scale = 1.0 / math.sqrt(slots * count * n_data * n_shard)
    tables = (slot_for, owner_mine, block_for, source_of)
    out_frames, grad_frames, grad_in, grad_out, small = module_call(
        scale, tables, frames, cotangent, limit, w_in, kernel, dw_gain[None], dw_bias[None], w_out, n_data)
    taps = kernel.shape[0]
    return (
        out_frames,
        grad_frames,
        grad_in,
        small[:taps],
        small[taps],
        small[taps + 1],
        grad_out,
    )


def solution(mesh):
    placed = (
        P(("dp", "fsdp"), None, None),
        P(),
        P(),
        P(),
        P("fsdp", None),
        P(),
        P(),
        P(),
        P("fsdp", None),
        P(("dp", "fsdp"), None, None),
    )
    return jax.shard_map(
        shards,
        mesh=mesh,
        in_specs=placed,
        out_specs=(
            P(("dp", "fsdp"), None, None),
            P(("dp", "fsdp"), None, None),
            P("fsdp", None),
            P(),
            P(),
            P(),
            P("fsdp", None),
        ),
        check_vma=False,
    )
```

time: 1570 us -> 148 us (0.09)
  waiting for transfers between devices: 1300 us -> 0 us
  Pallas kernels: 0 us -> 132 us
  blocking collectives: 123 us -> 0 us
  other arithmetic: 50.2 us -> 1.88 us
  matrix products: 30.9 us -> 0 us
  local copies, waits for them, and re-layouts: 34 us -> 11.9 us
    reduce_scatter x2 -> x0, waiting for transfers between devices: 1260 us -> none  [the longest x1 638 us: shards(): lax.psum_scatter(lax.dot_general(jnp.take(swish_flat, picked, axis=1), ma...]
    pallas_call x0 -> x1, Pallas kernels: none -> 132 us  [module_call(): pl.pallas_call(body, out_shape=tuple(outputs.values()), in_specs=[smem] *...]
    psum x1 -> x0, blocking collectives: 81 us -> none  [shards(): small_sums = lax.psum((d_kernel, d_gain, d_bias), ('dp', 'fsdp'))]
    all_gather x2 -> x0, blocking collectives: 41.8 us -> none  [the longest x1 21 us: shards(): lax.all_gather(share_in.astype(jnp.bfloat16), 'dp', axis=0, tiled=True)]
    dot_general x10 -> x0, matrix products: 30.9 us -> none  [the longest x1 5.62 us: shards(): lax.dot_general(jnp.take(xn_flat, picked, axis=1), dact_flat, contract, p...]
    all_to_all x2 -> x0, waiting for transfers between devices: 30 us -> none  [the longest x1 30 us: shards(): lax.all_to_all(route(outgoing, 'pj,jtd->ptd', frames), 'dp', split_axis=0...]
    reduce_sum x7 -> x3, other arithmetic: 24.7 us -> 1.88 us  [the longest x1 0.75 us: shards(): jnp.sum(jnp.where(matches, peers[None, :, None], 0), axis=(1, 2))]
    another operation x2 -> x0, other arithmetic: 17.5 us -> none
  transfers between devices with their start and end apart: 7 -> 0, of which waited for: 4 -> 0; matrix products, arithmetic and copies ran while one was open for 5% -> 0% of each run, Pallas kernels for 0% -> 0%
where the time goes in v1:
time: 148 us; the launch traced here: 146 us
  Pallas kernels  132 us (89%)
  local copies, waits for them, and re-layouts  11.9 us (8%)
  other arithmetic  1.88 us (1%)
    pallas_call x1, Pallas kernels, module_call(): pl.pallas_call(body, out_shape=tuple(outputs.values()), in_specs=[smem] *...  132 us
    unnamed x19, local copies, waits for them, and re-layouts  7.99 us

profile of v1, /device:TPU:0, one launch (start us, length us, event | category | flops | bytes accessed | tf_op | source)
XLA Modules:
  0.0 146.4 jit_solution(16387652717030205121)
XLA Ops:
  0.6 0.0 copy-start.3
  0.7 0.7 copy-done.3
  1.3 0.0 copy-start.4
  1.3 0.1 reshape.42
  1.4 0.6 copy-done.4
  2.0 0.1 reshape.45
  2.1 0.0 copy-start.6
  2.1 0.0 copy-start.5
  2.1 0.5 copy-done.6
  2.6 0.6 select_reduce_fusion.1.refs_2_
  3.2 0.7 broadcast_in_dim.52.refs_6_
  3.9 0.0 copy-done.5
  3.9 0.1 reshape.43
  4.0 0.1 copy.26
  4.1 0.1 copy.27
  4.1 0.5 select_reduce_fusion.2
  4.7 0.8 select_reduce_fusion.refs_3_
  5.4 131.9 %conv_module.1 = (bf16[8,64,1024]{2,1,0:T(8,128)(2,1)}, bf16[8,64,1024]{2,1,0:T(8,128)(2,1)}, f32[128,2048]{1,0:T(8,128)}, f32[128,1024]{1,0:T(8,128)}, f32[40,1024]{1,0:T(8,128)}) custom-call(s32[16]{0:T(128)} %get-tuple-element.17.refs_0_, s32[8]{0:T(128)} %copy-done.6, s32[16]{0:T(128)} %select_reduce_fusion.1.refs_2_, s32[8]{0:T(128)} %select_reduce_fusion.refs_3_, ...), custom_call_target="tpu_custom_call" | custom-call | tf_op jit(solution)/shard_map/conv_module/pallas_call | solution.py:596
  137.3 1.4 fusion.3
  138.7 1.6 %slice.9 = f32[31,1024]{1,0:T(8,128)} slice(f32[40,1024]{1,0:T(8,128)} %get-tuple-element.15), slice={[0:31], [0:1024]} | slice | bytes 253952 | tf_op jit(solution)/shard_map/slice | solution.py:644
  140.3 0.0 copy-start.1
  140.3 2.4 %copy.32 = bf16[8,64,1024]{2,1,0:T(8,128)(2,1)} copy(bf16[8,64,1024]{2,1,0:T(8,128)(2,1)} %get-tuple-element.32) | data formatting | bytes 2097152
  142.6 0.0 copy-done.1
  142.6 0.0 copy-start
  142.6 1.0 copy.33
  143.6 0.6 copy-done
  144.2 0.0 copy-start.2
  144.2 1.0 copy.34
  145.2 0.4 copy-done.2
  145.6 0.8 copy.35
  (2 shorter events, 0.0 us)
Async XLA Ops:
  0.6 0.7 copy-start.3
  1.3 0.7 copy-start.4
  2.1 0.5 copy-start.6
  2.1 1.8 %copy-start.5 = (s32[1024]{0:T(1024)S(1)}, s32[1024]{0:T(1024)}, u32[]{:S(2)}) copy-start(s32[1024]{0:T(1024)} %param.13) | copy-start | bytes 12292
  140.3 2.4 %copy-start.1 = (bf16[8,64,1024]{2,1,0:T(8,128)(2,1)S(1)}, bf16[8,64,1024]{2,1,0:T(8,128)(2,1)}, u32[]{:S(2)}) copy-start(bf16[8,64,1024]{2,1,0:T(8,128)(2,1)} %get-tuple-element.33) | copy-start | bytes 3145732
  142.6 1.6 %copy-start = (f32[128,2048]{1,0:T(8,128)S(1)}, f32[128,2048]{1,0:T(8,128)}, u32[]{:S(2)}) copy-start(f32[128,2048]{1,0:T(8,128)} %get-tuple-element.34) | copy-start | bytes 3145732
  144.2 1.4 copy-start.2

commit v2 on v1

--- a/solution.py
+++ b/solution.py
@@ -200,16 +200,17 @@
         m.dconv[pl.ds(half + i * steps, steps)] = dconv.reshape(steps, slots, width)
 
 
-def conv_back(m):
+def conv_back(m, side):
     rows, width = m.xn.shape
     taps, slots, _ = m.spread.shape
     frames = rows // slots
     half = (taps - 1) // 2
     steps = frames // CHUNK
-
-    @pl.loop(0, width // LANES * steps)
+    tiles = width // LANES // 2
+
+    @pl.loop(0, tiles * steps)
     def _(i):
-        l = i // steps
+        l = side * tiles + i // steps
         t = i % steps
         c = lanes_of(l)
         acc = slide(m.dconv, m.spread, t * CHUNK, c, True)
@@ -254,13 +255,17 @@
             m.small[l // 4, l % 4, pl.ds(taps + k, 1), :] = jnp.sum(m.sums[k, :, c], axis=0, keepdims=True)
 
 
-def norm_input_back(m):
-    rows, width = m.xn.shape
+def project_back(m):
+    width = m.xn.shape[1]
 
     @pl.loop(0, width // PIECE)
     def _(j):
         c = lanes_of(j, PIECE)
         m.wide[:, c] = lax.dot_general(m.da[...], m.w_in[c, :], NT, preferred_element_type=F32)
+
+
+def norm_input_back(m):
+    rows, width = m.xn.shape
 
     @pl.loop(0, rows // BLOCK)
     def _(i):
@@ -281,13 +286,14 @@
             m.pieces[core, k, y, a * RING + b] = part[low : low + size, :]
 
 
-def weight_in_grad(m):
+def weight_in_grad(m, side):
     @pl.loop(0, RING)
     def _(y):
         xn = m.xn[:, lanes_of(y, PIECE)]
-        for q in range(8):
-            part = lax.dot_general(xn, m.da[:, pl.ds(q * PIECE, PIECE)], TN, preferred_element_type=F32)
-            save_pieces(m, y, q % 2, q // 2, part.astype(BF16))
+        for b in range(RING):
+            cols = m.da[:, pl.ds((side * RING + b) * PIECE, PIECE)]
+            part = lax.dot_general(xn, cols, TN, preferred_element_type=F32)
+            save_pieces(m, y, side, b, part.astype(BF16))
 
 
 def weight_out_grad(m):
@@ -357,9 +363,22 @@
         m.w_in[mine, pl.ds((2 * j + 1) * PIECE, PIECE)] = m.w_in_shard[:, pl.ds(width + j * PIECE, PIECE)]
     m.w_out[mine, :] = m.w_out_shard[...]
 
+    n_shard = 2 * RING
+
+    def base(p):
+        return (p * n_shard + shard) * slots
+
     @pl.loop(0, n_data)
     def _(p):
-        m.sendb[p] = m.cot[m.slot_for[p]]
+        found, place, out_block = 0, 0, 0
+        for j in range(slots):
+            hit = m.owner[base(p) + j] == data
+            found = found + jnp.where(hit, 1, 0)
+            place = place + jnp.where(hit, m.slot[base(p) + j], 0)
+            out_block = out_block + jnp.where(m.owner[base(data) + j] == p, j, 0)
+        m.place[p] = place - slots * (1 - found)
+        m.block_for[p] = jnp.minimum(out_block, slots - 1)
+        m.sendb[p] = m.cot[jnp.minimum(place, slots - 1)]
 
     pl.semaphore_wait(barrier, 1 + len(ring_y) + len(ring_d))
 
@@ -370,10 +389,16 @@
         return m.w_out.at[r, :]
 
     weights, passed = [], []
-    for j in range(chunks + 1):
+    right, left = 1, RING - 1
+
+    def send_weights(j):
         src = part(j, y)
-        weights.append([push(src, src, m.weight_sems, (j, o - 1), peer_y(o)) for o in ring_y])
+        weights.append([push(src, src, m.weight_sems, (j, i), peer_y(o)) for i, o in enumerate((right, left))])
         passed.append([push(src, src, m.pass_sems, (j, 0), partner)])
+
+    ahead = 3
+    for j in range(ahead):
+        send_weights(j)
 
     def exchange(dst, sems):
         copies = [push(m.sendb.at[at_d(o)], dst.at[data], sems, o - 1, peer_d(o), False) for o in ring_d]
@@ -382,28 +407,48 @@
 
     cot_copies = exchange(m.cot_recv, m.cot_sems)
 
+    for b in range(slots):
+        m.limit[pl.ds(b, 1), :] = jnp.full((1, LANES), m.lengths[base(data) + b], jnp.int32)
     prepare(m)
     norm_input(m)
 
-    def weights_ready(j):
-        for o in ring_y:
-            weights[j][o - 1].wait_recv()
-            src = part(j, lax.rem(y + RING - o, RING))
-            passed[j].append(push(src, src, m.pass_sems, (j, o), partner))
+    @pl.loop(0, slots)
+    def _(s):
+        source = 0
+        for p in range(n_data):
+            source = source + jnp.where(m.place[p] == s, p, 0)
+        m.source_of[s] = jnp.minimum(source, n_data - 1)
+
+    def weights_near(j):
+        for i, (far, near) in enumerate(((left, right), (right, left))):
+            weights[j][i].wait_recv()
+            src = part(j, at_y(far))
+            piece = src.at[pl.ds(i * (per // 2), per // 2), :]
+            weights[j].append(push(piece, piece, m.weight_sems, (j, 2 + i), peer_y(near)))
+            passed[j].append(push(src, src, m.pass_sems, (j, 1 + i), partner))
+        if j + ahead <= chunks:
+            send_weights(j + ahead)
+
+    def weights_far(j):
+        arrive(weights[j][2:])
+        src = part(j, at_y(2))
+        passed[j].append(push(src, src, m.pass_sems, (j, 3), partner))
         arrive(passed[j])
 
+    weights_near(0)
     for j in range(chunks):
-        weights_ready(j)
+        weights_near(j + 1)
+        weights_far(j)
         gate_chunk(m, j)
         conv_chunk(m, j)
     norm_conv(m)
 
     arrive(cot_copies)
     for b in range(slots):
-        m.dx[pl.ds(b * frames, frames), :] = m.cot_recv[m.owner[b]]
+        m.dx[pl.ds(b * frames, frames), :] = m.cot_recv[m.owner[base(data) + b]]
     mask_cotangent(m)
 
-    weights_ready(chunks)
+    weights_far(chunks)
     mix_out(m)
     untime(m, m.lines)
     for copy in cot_copies:
@@ -475,7 +520,7 @@
                 piece = wide(m.fin[k, a * RING + b]) * scale
                 r = pl.ds(a * size, size)
                 if k < 2:
-                    m.grad_in[r, pl.ds((k * RING + b) * cols, cols)] = piece
+                    m.grad_in[r, pl.ds((b % 2 * RING + k * 2 + b // 2) * cols, cols)] = piece
                 else:
                     m.grad_out[r, pl.ds(b * cols, cols)] = piece
 
@@ -483,66 +528,73 @@
     two = core_start(2)
     norm_conv_back(m)
     two = first(2, two)
-    conv_back(m)
+    conv_back(m, 0)
+    weight_in_grad(m, 0)
+    zero = core_start(0)
     two = second(2, two)
+    conv_back(m, 1)
+    weight_in_grad(m, 1)
+    one = core_start(1)
+    zero = first(0, zero)
+    project_back(m)
+    one = first(1, one)
+    two = third(2, two)
     taps_back(m)
 
     small = [push(m.small.at[1 - core], m.small_core, m.small_sems, 0, partner)]
-    two = third(2, two)
-    weight_in_grad(m)
-    zero, one = core_start(0), core_start(1)
+    norm_input_back(m)
 
     arrive(small)
     m.small_core[...] = m.small_core[...] + m.small[core]
     m.small_y[y] = m.small_core[y]
     small = [push(m.small_core.at[at_y(o)], m.small_y.at[y], m.small_sems, o, peer_y(o)) for o in ring_y]
 
-    zero = first(0, zero)
-    one = first(1, one)
+    untime(m, m.grad_frames)
+    zero = second(0, zero)
 
     arrive(small)
     m.small_d[data] = (m.small_y[0] + m.small_y[1]) + (m.small_y[2] + m.small_y[3])
     small = [push(m.small_d.at[data], m.small_d.at[data], m.small_d_sems, o - 1, peer_d(o)) for o in ring_d]
 
-    norm_input_back(m)
-    untime(m, m.grad_frames)
+    arrive(out_copies)
+
+    @pl.loop(0, slots)
+    def _(s):
+        m.out_frames[s] = m.out_recv[m.source_of[s]]
+
     last(2, two)
+    one = second(1, one)
 
     arrive(small)
     total = m.small_d[0]
     for d in range(1, n_data):
         total = total + m.small_d[d]
     m.small_all[core, y] = total
-    mine = m.small_all.at[core, y]
-    small = [push(mine, mine, m.small_sems, RING + o, peer_y(o)) for o in ring_y]
-
-    zero = second(0, zero)
-    one = second(1, one)
+    own = m.small_all.at[core, y]
+    small = [push(own, own, m.small_sems, RING + o, peer_y(o)) for o in ring_y]
+
+    zero = third(0, zero)
+    one = third(1, one)
     arrive(small)
     half = m.small_all.at[core]
     small = [push(half, half, m.small_sems, 2 * RING, partner)]
-
-    zero = third(0, zero)
-    one = third(1, one)
-
-    arrive(out_copies)
-
-    @pl.loop(0, slots)
-    def _(s):
-        m.out_frames[s] = m.out_recv[m.source_of[s]]
+    last(0, zero)
+    last(1, one)
 
     arrive(small)
     lanes = m.small_all.shape[3]
+    taps = m.taps.shape[0]
     for a in range(2):
         for b in range(RING):
-            m.small_out[:, pl.ds((a * RING + b) * lanes, lanes)] = m.small_all[a, b] * scale
-    last(0, zero)
-    last(1, one)
+            c = pl.ds((a * RING + b) * lanes, lanes)
+            m.grad_taps[:, c] = m.small_all[a, b, pl.ds(0, taps), :] * scale
+            m.grad_gain[:, c] = m.small_all[a, b, pl.ds(taps, 1), :] * scale
+            m.grad_bias[:, c] = m.small_all[a, b, pl.ds(taps + 1, 1), :] * scale
     for copy in pending:
         copy.wait_send()
 
 
-def module_call(scale, tables, frames, cotangent, limit, w_in, taps, gain, bias, w_out, n_data):
+def module_call(scale, owner, slot, lengths, frames, cotangent, w_in, taps, gain, bias, w_out, n_data):
     slots, count, width = frames.shape
     rows = slots * count
     k = taps.shape[0]
@@ -552,16 +604,20 @@
     shape = jax.ShapeDtypeStruct
     dma = pltpu.SemaphoreType.DMA
     inputs = dict(
-        slot_for=tables[0], owner=tables[1], block_for=tables[2], source_of=tables[3],
-        x=frames.reshape(rows, width), cot=cotangent, limit=limit, w_in_shard=w_in, taps=taps,
+        owner=owner, slot=slot, lengths=lengths,
+        x=frames.reshape(rows, width), cot=cotangent, w_in_shard=w_in, taps=taps,
         gain=gain, bias=bias, w_out_shard=w_out)
     outputs = dict(
         out_frames=shape((slots, count, width), BF16),
         grad_frames=shape((slots, count, width), BF16),
         grad_in=shape((width // 8, 2 * width), F32),
         grad_out=shape((width // 8, width), F32),
-        small_out=shape((lines, width), F32))
+        grad_taps=shape((k, width), F32),
+        grad_gain=shape((1, width), F32),
+        grad_bias=shape((1, width), F32))
+    tables = dict(place=(n_data,), block_for=(n_data,), source_of=(slots,))
     buffers = dict(
+        limit=((slots, LANES), jnp.int32),
         w_in=((width, 2 * width), BF16), w_out=((width, width), BF16),
         xp=((rows, width), BF16), xn=((rows, width), BF16), sig=((rows, width), F32),
         chat=((rows, width), F32), rstd=((rows, LANES), F32), sw=((rows, width), BF16),
@@ -581,10 +637,10 @@
         small_y=((RING, lines, lanes), F32), small_d=((n_data, lines, lanes), F32),
         small_all=((2, RING, lines, lanes), F32))
     pairs = dict(
-        weight_sems=(5, RING - 1), pass_sems=(5, RING), cot_sems=(n_data - 1,), out_sems=(n_data - 1,),
+        weight_sems=(5, 4), pass_sems=(5, RING), cot_sems=(n_data - 1,), out_sems=(n_data - 1,),
         core_sems=(3,), sum_y_sems=(3, RING - 1), sum_d_sems=(3, n_data - 1), fin_sems=(3, n_data - 1),
         small_sems=(2 * RING + 1,), small_d_sems=(n_data - 1,))
-    names = list(inputs) + list(outputs) + list(buffers)
+    names = list(inputs) + list(outputs) + list(tables) + list(buffers)
     vmem = pl.BlockSpec(memory_space=pltpu.VMEM)
     smem = pl.BlockSpec(memory_space=pltpu.SMEM)
 
@@ -596,9 +652,10 @@
     return pl.pallas_call(
         body,
         out_shape=tuple(outputs.values()),
-        in_specs=[smem] * 4 + [vmem] * (len(inputs) - 4),
+        in_specs=[smem] * 3 + [vmem] * (len(inputs) - 3),
         out_specs=(vmem,) * len(outputs),
-        scratch_shapes=[pltpu.VMEM(*b) for b in buffers.values()]
+        scratch_shapes=[pltpu.SMEM(t, jnp.int32) for t in tables.values()]
+        + [pltpu.VMEM(*b) for b in buffers.values()]
         + [dma(s) for s in pairs.values() for _ in range(2)],
         compiler_params=pltpu.CompilerParams(
             collective_id=0, has_side_effects=True, vmem_limit_bytes=VMEM_LIMIT),
@@ -612,38 +669,18 @@
 def shards(frames, lengths, owner, slot, w_in, kernel, dw_gain, dw_bias, w_out, cotangent):
     n_data = lax.axis_size("dp")
     n_shard = lax.axis_size("fsdp")
-    my_data = lax.axis_index("dp")
-    my_shard = lax.axis_index("fsdp")
     slots, count, width = frames.shape
-
-    def column_of(table):
-        grid = table.reshape(n_data, n_shard, slots)
-        return lax.dynamic_index_in_dim(grid, my_shard, 1, keepdims=False)
-
-    owner_col = column_of(owner)
-    slot_col = column_of(slot)
-    owner_mine = lax.dynamic_index_in_dim(owner_col, my_data, 0, keepdims=False)
-    length_mine = lax.dynamic_index_in_dim(column_of(lengths), my_data, 0, keepdims=False)
-    here = owner_col == my_data
-    slot_for = jnp.sum(jnp.where(here, slot_col, 0), axis=1)
-    slot_ids = jnp.arange(slots, dtype=jnp.int32)
-    peers = jnp.arange(n_data, dtype=jnp.int32)
-    block_for = jnp.sum(jnp.where(owner_mine[None, :] == peers[:, None], slot_ids[None, :], 0), axis=1)
-    matches = here[None, :, :] & (slot_col[None, :, :] == slot_ids[:, None, None])
-    source_of = jnp.sum(jnp.where(matches, peers[None, :, None], 0), axis=(1, 2))
-    limit = jnp.broadcast_to(length_mine[:, None], (slots, LANES))
     scale = 1.0 / math.sqrt(slots * count * n_data * n_shard)
-    tables = (slot_for, owner_mine, block_for, source_of)
-    out_frames, grad_frames, grad_in, grad_out, small = module_call(
-        scale, tables, frames, cotangent, limit, w_in, kernel, dw_gain[None], dw_bias[None], w_out, n_data)
-    taps = kernel.shape[0]
+    out_frames, grad_frames, grad_in, grad_out, grad_taps, grad_gain, grad_bias = module_call(
+        scale, owner, slot, lengths, frames, cotangent, w_in, kernel, dw_gain[None], dw_bias[None], w_out,
+        n_data)
     return (
         out_frames,
         grad_frames,
         grad_in,
-        small[:taps],
-        small[taps],
-        small[taps + 1],
+        grad_taps,
+        grad_gain[0],
+        grad_bias[0],
         grad_out,
     )
 

time: 148 us -> 129 us (0.87)
  Pallas kernels: 132 us -> 119 us
  local copies, waits for them, and re-layouts: 11.9 us -> 7.69 us
  other arithmetic: 1.88 us -> 0 us
    pallas_call x1, Pallas kernels: 132 us -> 119 us  [module_call(): pl.pallas_call(body, out_shape=tuple(outputs.values()), in_specs=[smem] *...]
    slice x2 -> x0, local copies, waits for them, and re-layouts: 2.94 us -> none  [the longest x1 1.57 us: shards(): small[:taps]]
    reduce_sum x3 -> x0, other arithmetic: 1.88 us -> none  [the longest x1 0.75 us: shards(): jnp.sum(jnp.where(matches, peers[None, :, None], 0), axis=(1, 2))]
where the time goes in v2:
time: 129 us; the launch traced here: 127 us
  Pallas kernels  119 us (92%)
  local copies, waits for them, and re-layouts  7.69 us (6%)
    pallas_call x1, Pallas kernels, module_call(): pl.pallas_call(body, out_shape=tuple(outputs.values()), in_specs=[smem] *...  119 us
    unnamed x19, local copies, waits for them, and re-layouts  7.69 us

profile of v2, /device:TPU:0, one launch (start us, length us, event | category | flops | bytes accessed | tf_op | source)
XLA Modules:
  0.0 127.4 jit_solution(7123136704129563625)
XLA Ops:
  0.6 119.1 %conv_module.1 = (bf16[8,64,1024]{2,1,0:T(8,128)(2,1)}, bf16[8,64,1024]{2,1,0:T(8,128)(2,1)}, f32[128,2048]{1,0:T(8,128)}, f32[128,1024]{1,0:T(8,128)}, f32[31,1...) custom-call(s32[1024]{0:T(1024)} %refs_0_.1, s32[1024]{0:T(1024)} %refs_1_.1, s32[1024]{0:T(1024)} %refs_2_.1, ...), custom_call_target="tpu_custom_call" | custom-call | tf_op jit(solution)/shard_map/conv_module/pallas_call | solution.py:652
  119.7 0.0 copy-start.1
  119.7 2.4 %copy.24 = bf16[8,64,1024]{2,1,0:T(8,128)(2,1)} copy(bf16[8,64,1024]{2,1,0:T(8,128)(2,1)} %get-tuple-element.28) | data formatting | bytes 2097152
  122.1 0.0 copy-done.1
  122.1 0.0 copy-start
  122.1 1.0 copy.25
  123.1 0.6 copy-done
  123.7 0.0 copy-start.3
  123.7 0.0 copy-start.2
  123.7 1.0 copy.26
  124.7 0.0 copy-done.3
  124.7 0.0 copy-start.5
  124.7 0.7 copy.27
  125.3 0.0 copy-done.5
  125.4 0.0 copy-start.4
  125.4 0.6 copy.28
  126.0 0.1 copy-done.4
  126.0 0.6 copy.29
  126.6 0.0 copy-done.2
  126.6 0.8 copy.30
Async XLA Ops:
  119.7 2.4 %copy-start.1 = (bf16[8,64,1024]{2,1,0:T(8,128)(2,1)S(1)}, bf16[8,64,1024]{2,1,0:T(8,128)(2,1)}, u32[]{:S(2)}) copy-start(bf16[8,64,1024]{2,1,0:T(8,128)(2,1)} %get-tuple-element.29) | copy-start | bytes 3145732
  122.1 1.6 %copy-start = (f32[128,2048]{1,0:T(8,128)S(1)}, f32[128,2048]{1,0:T(8,128)}, u32[]{:S(2)}) copy-start(f32[128,2048]{1,0:T(8,128)} %get-tuple-element.30) | copy-start | bytes 3145732
  123.7 1.0 copy-start.3
  123.7 2.9 %copy-start.2 = (f32[128,1024]{1,0:T(8,128)S(1)}, f32[128,1024]{1,0:T(8,128)}, u32[]{:S(2)}) copy-start(f32[128,1024]{1,0:T(8,128)} %get-tuple-element.34) | copy-start | bytes 1572868
  124.7 0.7 copy-start.5
  125.4 0.7 copy-start.4

commit v3 on v2

--- a/solution.py
+++ b/solution.py
@@ -471,44 +471,27 @@
         def _(a):
             m.pieces[core, k, a] = (wide(m.pieces[core, k, a]) + wide(m.core_recv[k, a])).astype(BF16)
 
-        if k != 1:
-            return [push(m.pieces.at[core, k, at_y(o)], m.recv_y.at[k // 2, o - 1], m.sum_y_sems,
-                         (k, o - 1), peer_y(o)) for o in ring_y]
-        return [push(m.pieces.at[core, k, :, at_d(o)], m.recv_d.at[o - 1], m.sum_d_sems,
-                     (k, o - 1), peer_d(o)) for o in ring_d]
+        return [push(m.pieces.at[core, k, at_y(o)], m.recv_y.at[k, o - 1], m.sum_y_sems,
+                     (k, o - 1), peer_y(o)) for o in ring_y]
 
     def second(k, copies):
         arrive(copies)
-        if k != 1:
-            @pl.loop(0, n_data)
-            def _(d):
-                acc = wide(m.pieces[core, k, y, d])
-                for o in ring_y:
-                    acc = acc + wide(m.recv_y[k // 2, o - 1, d])
-                m.pieces[core, k, y, d] = acc.astype(BF16)
-
-            return [push(m.pieces.at[core, k, y, at_d(o)], m.last_d.at[k // 2, o - 1], m.sum_d_sems,
-                         (k, o - 1), peer_d(o)) for o in ring_d]
-
-        @pl.loop(0, RING)
-        def _(a):
-            acc = wide(m.pieces[core, k, a, data])
-            for o in ring_d:
-                acc = acc + wide(m.recv_d[o - 1, a])
-            m.pieces[core, k, a, data] = acc.astype(BF16)
-
-        return [push(m.pieces.at[core, k, at_y(o), data], m.last_y.at[o - 1], m.sum_y_sems,
-                     (k, o - 1), peer_y(o)) for o in ring_y]
+
+        @pl.loop(0, n_data)
+        def _(d):
+            acc = wide(m.pieces[core, k, y, d])
+            for o in ring_y:
+                acc = acc + wide(m.recv_y[k, o - 1, d])
+            m.pieces[core, k, y, d] = acc.astype(BF16)
+
+        return [push(m.pieces.at[core, k, y, at_d(o)], m.last_d.at[k, o - 1], m.sum_d_sems,
+                     (k, o - 1), peer_d(o)) for o in ring_d]
 
     def third(k, copies):
         arrive(copies)
         acc = wide(m.pieces[core, k, y, data])
-        if k != 1:
-            for o in ring_d:
-                acc = acc + wide(m.last_d[k // 2, o - 1])
-        else:
-            for o in ring_y:
-                acc = acc + wide(m.last_y[o - 1])
+        for o in ring_d:
+            acc = acc + wide(m.last_d[k, o - 1])
         m.fin[k, data] = acc.astype(BF16)
         return [push(m.fin.at[k, data], m.fin.at[k, data], m.fin_sems, (k, o - 1), peer_d(o)) for o in ring_d]
 
@@ -629,9 +612,8 @@
         cot_recv=((n_data, count, width), BF16), out_recv=((n_data, count, width), BF16),
         pieces=((2, 3, RING, n_data, size, cols), BF16),
         core_recv=((3, RING, n_data, size, cols), BF16),
-        recv_y=((2, RING - 1, n_data, size, cols), BF16),
-        recv_d=((n_data - 1, RING, size, cols), BF16),
-        last_d=((2, n_data - 1, size, cols), BF16), last_y=((RING - 1, size, cols), BF16),
+        recv_y=((3, RING - 1, n_data, size, cols), BF16),
+        last_d=((3, n_data - 1, size, cols), BF16),
         fin=((3, n_data, size, cols), BF16),
         small=((2, RING, lines, lanes), F32), small_core=((RING, lines, lanes), F32),
         small_y=((RING, lines, lanes), F32), small_d=((n_data, lines, lanes), F32),
@@ -666,14 +648,44 @@
 VMEM_LIMIT = 63 * 2**20
 
 
+def finish_kernel(*refs):
+    count = len(refs) // 4
+    plain, sems = refs[: 3 * count], refs[3 * count :]
+    loads, stores = [], []
+    for i in range(count):
+        loads.append(pltpu.make_async_copy(plain[i], plain[2 * count + i], sems[i].at[0]))
+        loads[-1].start()
+    for i in range(count):
+        loads[i].wait()
+        stores.append(pltpu.make_async_copy(plain[2 * count + i], plain[count + i], sems[i].at[1]))
+        stores[-1].start()
+    for copy in stores:
+        copy.wait()
+
+
+def finish(arrays):
+    hbm = pl.BlockSpec(memory_space=pl.ANY)
+    return pl.pallas_call(
+        finish_kernel,
+        out_shape=tuple(jax.ShapeDtypeStruct(a.shape, a.dtype) for a in arrays),
+        in_specs=[hbm] * len(arrays),
+        out_specs=(hbm,) * len(arrays),
+        scratch_shapes=[pltpu.VMEM(a.shape, a.dtype) for a in arrays]
+        + [pltpu.SemaphoreType.DMA((2,)) for _ in arrays],
+        compiler_params=pltpu.CompilerParams(vmem_limit_bytes=VMEM_LIMIT),
+        name="finish",
+    )(*arrays)
+
+
 def shards(frames, lengths, owner, slot, w_in, kernel, dw_gain, dw_bias, w_out, cotangent):
     n_data = lax.axis_size("dp")
     n_shard = lax.axis_size("fsdp")
     slots, count, width = frames.shape
     scale = 1.0 / math.sqrt(slots * count * n_data * n_shard)
-    out_frames, grad_frames, grad_in, grad_out, grad_taps, grad_gain, grad_bias = module_call(
+    results = module_call(
         scale, owner, slot, lengths, frames, cotangent, w_in, kernel, dw_gain[None], dw_bias[None], w_out,
         n_data)
+    out_frames, grad_frames, grad_in, grad_out, grad_taps, grad_gain, grad_bias = finish(results)
     return (
         out_frames,
         grad_frames,

time: 129 us -> 126 us (0.977); the launches traced: 127 us -> 126 us
  local copies, waits for them, and re-layouts: 7.69 us -> 0 us
  Pallas kernels: 119 us -> 126 us
    unnamed x19 -> x0, local copies, waits for them, and re-layouts: 7.69 us -> none
    pallas_call x1, Pallas kernels: 119 us -> 122 us  [module_call(): pl.pallas_call(body, out_shape=tuple(outputs.values()), in_specs=[smem] *...]
    pallas_call x0 -> x1, Pallas kernels: none -> 3.22 us  [finish(): pl.pallas_call(finish_kernel, out_shape=tuple((jax.ShapeDtypeStruct(a.sha...]
where the time goes in v3:
time: 126 us
  Pallas kernels  126 us (100%)
    pallas_call x1, Pallas kernels, module_call(): pl.pallas_call(body, out_shape=tuple(outputs.values()), in_specs=[smem] *...  122 us
    pallas_call x1, Pallas kernels, finish(): pl.pallas_call(finish_kernel, out_shape=tuple((jax.ShapeDtypeStruct(a.sha...  3.22 us

profile of v3, /device:TPU:0, one launch (start us, length us, event | category | flops | bytes accessed | tf_op | source)
XLA Modules:
  0.0 126.2 jit_solution(10651204742053244607)
XLA Ops:
  0.6 122.4 %conv_module.1 = (bf16[8,64,1024]{2,1,0:T(8,128)(2,1)}, bf16[8,64,1024]{2,1,0:T(8,128)(2,1)}, f32[128,2048]{1,0:T(8,128)}, f32[128,1024]{1,0:T(8,128)}, f32[31,1...) custom-call(s32[1024]{0:T(1024)} %refs_0_.1, s32[1024]{0:T(1024)} %refs_1_.1, s32[1024]{0:T(1024)} %refs_2_.1, ...), custom_call_target="tpu_custom_call" | custom-call | tf_op jit(solution)/shard_map/conv_module/pallas_call | solution.py:634
  123.0 3.2 %finish.1 = (bf16[8,64,1024]{2,1,0:T(8,128)(2,1)}, bf16[8,64,1024]{2,1,0:T(8,128)(2,1)}, f32[128,2048]{1,0:T(8,128)}, f32[128,1024]{1,0:T(8,128)}, f32[31,1024]{...) custom-call(bf16[8,64,1024]{2,1,0:T(8,128)(2,1)} %get-tuple-element.21.refs_0_, ...), custom_call_target="tpu_custom_call" | custom-call | tf_op jit(solution)/shard_map/finish/pallas_call | solution.py:668

commit v4 on v3

--- a/solution.py
+++ b/solution.py
@@ -368,6 +368,26 @@
     def base(p):
         return (p * n_shard + shard) * slots
 
+    pl.semaphore_wait(barrier, 1 + len(ring_y) + len(ring_d))
+
+    def part(j, owner_y):
+        r = pl.ds(pl.multiple_of((owner_y * 2 + core) * per, per), per)
+        if j < chunks:
+            return m.w_in.at[r, pl.ds(2 * j * PIECE, 2 * PIECE)]
+        return m.w_out.at[r, :]
+
+    weights, passed = [], []
+    right, left = 1, RING - 1
+
+    def send_weights(j):
+        src = part(j, y)
+        weights.append([push(src, src, m.weight_sems, (j, i), peer_y(o)) for i, o in enumerate((right, left))])
+        passed.append([push(src, src, m.pass_sems, (j, 0), partner)])
+
+    ahead = 3
+    for j in range(ahead):
+        send_weights(j)
+
     @pl.loop(0, n_data)
     def _(p):
         found, place, out_block = 0, 0, 0
@@ -380,26 +400,6 @@
         m.block_for[p] = jnp.minimum(out_block, slots - 1)
         m.sendb[p] = m.cot[jnp.minimum(place, slots - 1)]
 
-    pl.semaphore_wait(barrier, 1 + len(ring_y) + len(ring_d))
-
-    def part(j, owner_y):
-        r = pl.ds(pl.multiple_of((owner_y * 2 + core) * per, per), per)
-        if j < chunks:
-            return m.w_in.at[r, pl.ds(2 * j * PIECE, 2 * PIECE)]
-        return m.w_out.at[r, :]
-
-    weights, passed = [], []
-    right, left = 1, RING - 1
-
-    def send_weights(j):
-        src = part(j, y)
-        weights.append([push(src, src, m.weight_sems, (j, i), peer_y(o)) for i, o in enumerate((right, left))])
-        passed.append([push(src, src, m.pass_sems, (j, 0), partner)])
-
-    ahead = 3
-    for j in range(ahead):
-        send_weights(j)
-
     def exchange(dst, sems):
         copies = [push(m.sendb.at[at_d(o)], dst.at[data], sems, o - 1, peer_d(o), False) for o in ring_d]
         dst[data] = m.sendb[data]
@@ -442,24 +442,6 @@
         gate_chunk(m, j)
         conv_chunk(m, j)
     norm_conv(m)
-
-    arrive(cot_copies)
-    for b in range(slots):
-        m.dx[pl.ds(b * frames, frames), :] = m.cot_recv[m.owner[base(data) + b]]
-    mask_cotangent(m)
-
-    weights_far(chunks)
-    mix_out(m)
-    untime(m, m.lines)
-    for copy in cot_copies:
-        copy.wait_send()
-
-    @pl.loop(0, n_data)
-    def _(p):
-        m.sendb[p] = m.lines[m.block_for[p]]
-
-    out_copies = exchange(m.out_recv, m.out_sems)
-    pending.extend(out_copies)
 
     def core_start(k):
         return [push(m.pieces.at[1 - core, k], m.core_recv.at[k], m.core_sems, k, partner)]
@@ -507,46 +489,65 @@
                 else:
                     m.grad_out[r, pl.ds(b * cols, cols)] = piece
 
+    arrive(cot_copies)
+    for b in range(slots):
+        m.dx[pl.ds(b * frames, frames), :] = m.cot_recv[m.owner[base(data) + b]]
+    mask_cotangent(m)
+
     weight_out_grad(m)
     two = core_start(2)
+    weights_far(chunks)
+    mix_out(m)
+    two = first(2, two)
+    untime(m, m.lines)
+    for copy in cot_copies:
+        copy.wait_send()
+
+    @pl.loop(0, n_data)
+    def _(p):
+        m.sendb[p] = m.lines[m.block_for[p]]
+
+    out_copies = exchange(m.out_recv, m.out_sems)
+    pending.extend(out_copies)
+
     norm_conv_back(m)
-    two = first(2, two)
     conv_back(m, 0)
     weight_in_grad(m, 0)
     zero = core_start(0)
     two = second(2, two)
+    zero = first(0, zero)
     conv_back(m, 1)
     weight_in_grad(m, 1)
     one = core_start(1)
-    zero = first(0, zero)
+    two = third(2, two)
     project_back(m)
     one = first(1, one)
-    two = third(2, two)
     taps_back(m)
 
     small = [push(m.small.at[1 - core], m.small_core, m.small_sems, 0, partner)]
     norm_input_back(m)
-
     arrive(small)
     m.small_core[...] = m.small_core[...] + m.small[core]
     m.small_y[y] = m.small_core[y]
     small = [push(m.small_core.at[at_y(o)], m.small_y.at[y], m.small_sems, o, peer_y(o)) for o in ring_y]
 
+    zero = second(0, zero)
     untime(m, m.grad_frames)
-    zero = second(0, zero)
+    last(2, two)
+    arrive(out_copies)
+
+    @pl.loop(0, slots)
+    def _(s):
+        m.out_frames[s] = m.out_recv[m.source_of[s]]
+
+    zero = third(0, zero)
+    one = second(1, one)
 
     arrive(small)
     m.small_d[data] = (m.small_y[0] + m.small_y[1]) + (m.small_y[2] + m.small_y[3])
     small = [push(m.small_d.at[data], m.small_d.at[data], m.small_d_sems, o - 1, peer_d(o)) for o in ring_d]
-
-    arrive(out_copies)
-
-    @pl.loop(0, slots)
-    def _(s):
-        m.out_frames[s] = m.out_recv[m.source_of[s]]
-
-    last(2, two)
-    one = second(1, one)
+    last(0, zero)
+    one = third(1, one)
 
     arrive(small)
     total = m.small_d[0]
@@ -555,13 +556,9 @@
     m.small_all[core, y] = total
     own = m.small_all.at[core, y]
     small = [push(own, own, m.small_sems, RING + o, peer_y(o)) for o in ring_y]
-
-    zero = third(0, zero)
-    one = third(1, one)
     arrive(small)
     half = m.small_all.at[core]
     small = [push(half, half, m.small_sems, 2 * RING, partner)]
-    last(0, zero)
     last(1, one)
 
     arrive(small)

time: 126 us -> 134 us (1.063); the launches traced: 126 us -> 132 us
  Pallas kernels: 126 us -> 131 us
    pallas_call x1, Pallas kernels: 122 us -> 128 us  [module_call(): pl.pallas_call(body, out_shape=tuple(outputs.values()), in_specs=[smem] *...]
where the time goes in v4:
time: 134 us; the launch traced here: 132 us
  Pallas kernels  131 us (98%)
    pallas_call x1, Pallas kernels, module_call(): pl.pallas_call(body, out_shape=tuple(outputs.values()), in_specs=[smem] *...  128 us
    pallas_call x1, Pallas kernels, finish(): pl.pallas_call(finish_kernel, out_shape=tuple((jax.ShapeDtypeStruct(a.sha...  3.22 us

profile of v4, /device:TPU:0, one launch (start us, length us, event | category | flops | bytes accessed | tf_op | source)
XLA Modules:
  0.0 131.9 jit_solution(12814414173681311415)
XLA Ops:
  0.6 128.1 %conv_module.1 = (bf16[8,64,1024]{2,1,0:T(8,128)(2,1)}, bf16[8,64,1024]{2,1,0:T(8,128)(2,1)}, f32[128,2048]{1,0:T(8,128)}, f32[128,1024]{1,0:T(8,128)}, f32[31,1...) custom-call(s32[1024]{0:T(1024)} %refs_0_.1, s32[1024]{0:T(1024)} %refs_1_.1, s32[1024]{0:T(1024)} %refs_2_.1, ...), custom_call_target="tpu_custom_call" | custom-call | tf_op jit(solution)/shard_map/conv_module/pallas_call | solution.py:631
  128.7 3.2 %finish.1 = (bf16[8,64,1024]{2,1,0:T(8,128)(2,1)}, bf16[8,64,1024]{2,1,0:T(8,128)(2,1)}, f32[128,2048]{1,0:T(8,128)}, f32[128,1024]{1,0:T(8,128)}, f32[31,1024]{...) custom-call(bf16[8,64,1024]{2,1,0:T(8,128)(2,1)} %get-tuple-element.21.refs_0_, ...), custom_call_target="tpu_custom_call" | custom-call | tf_op jit(solution)/shard_map/finish/pallas_call | solution.py:665

commit v5 on v4

--- a/solution.py
+++ b/solution.py
@@ -368,26 +368,6 @@
     def base(p):
         return (p * n_shard + shard) * slots
 
-    pl.semaphore_wait(barrier, 1 + len(ring_y) + len(ring_d))
-
-    def part(j, owner_y):
-        r = pl.ds(pl.multiple_of((owner_y * 2 + core) * per, per), per)
-        if j < chunks:
-            return m.w_in.at[r, pl.ds(2 * j * PIECE, 2 * PIECE)]
-        return m.w_out.at[r, :]
-
-    weights, passed = [], []
-    right, left = 1, RING - 1
-
-    def send_weights(j):
-        src = part(j, y)
-        weights.append([push(src, src, m.weight_sems, (j, i), peer_y(o)) for i, o in enumerate((right, left))])
-        passed.append([push(src, src, m.pass_sems, (j, 0), partner)])
-
-    ahead = 3
-    for j in range(ahead):
-        send_weights(j)
-
     @pl.loop(0, n_data)
     def _(p):
         found, place, out_block = 0, 0, 0
@@ -400,6 +380,26 @@
         m.block_for[p] = jnp.minimum(out_block, slots - 1)
         m.sendb[p] = m.cot[jnp.minimum(place, slots - 1)]
 
+    pl.semaphore_wait(barrier, 1 + len(ring_y) + len(ring_d))
+
+    def part(j, owner_y):
+        r = pl.ds(pl.multiple_of((owner_y * 2 + core) * per, per), per)
+        if j < chunks:
+            return m.w_in.at[r, pl.ds(2 * j * PIECE, 2 * PIECE)]
+        return m.w_out.at[r, :]
+
+    weights, passed = [], []
+    right, left = 1, RING - 1
+
+    def send_weights(j):
+        src = part(j, y)
+        weights.append([push(src, src, m.weight_sems, (j, i), peer_y(o)) for i, o in enumerate((right, left))])
+        passed.append([push(src, src, m.pass_sems, (j, 0), partner)])
+
+    ahead = 3
+    for j in range(ahead):
+        send_weights(j)
+
     def exchange(dst, sems):
         copies = [push(m.sendb.at[at_d(o)], dst.at[data], sems, o - 1, peer_d(o), False) for o in ring_d]
         dst[data] = m.sendb[data]
@@ -519,7 +519,6 @@
     conv_back(m, 1)
     weight_in_grad(m, 1)
     one = core_start(1)
-    two = third(2, two)
     project_back(m)
     one = first(1, one)
     taps_back(m)
@@ -533,7 +532,7 @@
 
     zero = second(0, zero)
     untime(m, m.grad_frames)
-    last(2, two)
+    two = third(2, two)
     arrive(out_copies)
 
     @pl.loop(0, slots)
@@ -546,6 +545,7 @@
     arrive(small)
     m.small_d[data] = (m.small_y[0] + m.small_y[1]) + (m.small_y[2] + m.small_y[3])
     small = [push(m.small_d.at[data], m.small_d.at[data], m.small_d_sems, o - 1, peer_d(o)) for o in ring_d]
+    last(2, two)
     last(0, zero)
     one = third(1, one)
 

time: 134 us -> 117 us (0.87)
  Pallas kernels: 131 us -> 115 us
    pallas_call x1, Pallas kernels: 128 us -> 112 us  [module_call(): pl.pallas_call(body, out_shape=tuple(outputs.values()), in_specs=[smem] *...]
where the time goes in v5:
time: 117 us; the launch traced here: 116 us
  Pallas kernels  115 us (98%)
    pallas_call x1, Pallas kernels, module_call(): pl.pallas_call(body, out_shape=tuple(outputs.values()), in_specs=[smem] *...  112 us
    pallas_call x1, Pallas kernels, finish(): pl.pallas_call(finish_kernel, out_shape=tuple((jax.ShapeDtypeStruct(a.sha...  3.22 us

profile of v5, /device:TPU:0, one launch (start us, length us, event | category | flops | bytes accessed | tf_op | source)
XLA Modules:
  0.0 115.8 jit_solution(2131632864630052828)
XLA Ops:
  0.6 112.0 %conv_module.1 = (bf16[8,64,1024]{2,1,0:T(8,128)(2,1)}, bf16[8,64,1024]{2,1,0:T(8,128)(2,1)}, f32[128,2048]{1,0:T(8,128)}, f32[128,1024]{1,0:T(8,128)}, f32[31,1...) custom-call(s32[1024]{0:T(1024)} %refs_0_.1, s32[1024]{0:T(1024)} %refs_1_.1, s32[1024]{0:T(1024)} %refs_2_.1, ...), custom_call_target="tpu_custom_call" | custom-call | tf_op jit(solution)/shard_map/conv_module/pallas_call | solution.py:631
  112.6 3.2 %finish.1 = (bf16[8,64,1024]{2,1,0:T(8,128)(2,1)}, bf16[8,64,1024]{2,1,0:T(8,128)(2,1)}, f32[128,2048]{1,0:T(8,128)}, f32[128,1024]{1,0:T(8,128)}, f32[31,1024]{...) custom-call(bf16[8,64,1024]{2,1,0:T(8,128)(2,1)} %get-tuple-element.21.refs_0_, ...), custom_call_target="tpu_custom_call" | custom-call | tf_op jit(solution)/shard_map/finish/pallas_call | solution.py:665

commit v6 on v5

--- a/solution.py
+++ b/solution.py
@@ -13,7 +13,7 @@
 LANES = 128
 CHUNK = 16
 PIECE = 256
-BLOCK = 64
+BLOCK = 128
 RING = 4
 EPS = 1e-05
 NT = (((1,), (1,)), ((), ()))

time: 117 us -> 117 us (level)
  no operation moved by 1% of the time
where the time goes in v6:
time: 117 us; the launch traced here: 115 us
  Pallas kernels  115 us (98%)
    pallas_call x1, Pallas kernels, module_call(): pl.pallas_call(body, out_shape=tuple(outputs.values()), in_specs=[smem] *...  111 us
    pallas_call x1, Pallas kernels, finish(): pl.pallas_call(finish_kernel, out_shape=tuple((jax.ShapeDtypeStruct(a.sha...  3.22 us

profile of v6, /device:TPU:0, one launch (start us, length us, event | category | flops | bytes accessed | tf_op | source)
XLA Modules:
  0.0 115.2 jit_solution(13985519322741199122)
XLA Ops:
  0.6 111.3 %conv_module.1 = (bf16[8,64,1024]{2,1,0:T(8,128)(2,1)}, bf16[8,64,1024]{2,1,0:T(8,128)(2,1)}, f32[128,2048]{1,0:T(8,128)}, f32[128,1024]{1,0:T(8,128)}, f32[31,1...) custom-call(s32[1024]{0:T(1024)} %refs_0_.1, s32[1024]{0:T(1024)} %refs_1_.1, s32[1024]{0:T(1024)} %refs_2_.1, ...), custom_call_target="tpu_custom_call" | custom-call | tf_op jit(solution)/shard_map/conv_module/pallas_call | solution.py:631
  112.0 3.2 %finish.1 = (bf16[8,64,1024]{2,1,0:T(8,128)(2,1)}, bf16[8,64,1024]{2,1,0:T(8,128)(2,1)}, f32[128,2048]{1,0:T(8,128)}, f32[128,1024]{1,0:T(8,128)}, f32[31,1024]{...) custom-call(bf16[8,64,1024]{2,1,0:T(8,128)(2,1)} %get-tuple-element.21.refs_0_, ...), custom_call_target="tpu_custom_call" | custom-call | tf_op jit(solution)/shard_map/finish/pallas_call | solution.py:665
